TPU v7x, 256 devices: a whole 4x4x8 slice. The times are simulated.
256 devices in a mesh: src: 8 (over y, core), tgt: 32 (over z, x).
Axes of the slice: x: 4, y: 4, z: 8, core: 2. Of those that a mesh axis runs over, the one named last changes fastest.
Arguments:
- src_embed: bfloat16 [8192, 256], P('src'), may hold values from -128 to 128
- tgt_embed: bfloat16 [155648, 256], P('tgt'), may hold values from -1 to 1
- qwen_embed: bfloat16 [155648, 256], P('tgt'), may hold values from -6 to 6
- other_log: float32 [155648], P('tgt'), may hold values from -12 to -10
- src_counts: int32 [8192], P('src'), may hold values from 1 to 999
- tgt_counts: int32 [155648], P('tgt'), may hold values from 1 to 999
Outputs:
- transported: float32 [8192, 256], P(('src', 'tgt'))
All inputs are finite; a program needn't handle non-finite values.
Results may differ from a plain program's by a relative error of at most 0.0034.
Values sent between devices are 32-bit elements; how exact they have to be, the bound alone decides.
A program may use at most 128 MiB of HBM per device.

v0:
```python
import jax
import jax.numpy as jnp
from jax import lax
from jax.sharding import PartitionSpec as P

ITERS = 2
inv_temp = 4.0


def logits_of(src_embed, tgt_embed):
    products = lax.dot_general(
        src_embed, tgt_embed, (((1,), (1,)), ((), ())), preferred_element_type=jnp.float32
    )
    return products * inv_temp


def row_lse(values):
    local_peak = jnp.max(values, axis=1)
    peak = lax.pmax(local_peak, "tgt")
    total = lax.psum(jnp.sum(jnp.exp(values - peak[:, None]), axis=1), "tgt")
    return peak + jnp.log(total)


def col_lse(values):
    local_peak = jnp.max(values, axis=0)
    peak = lax.pmax(local_peak, "src")
    total = lax.psum(jnp.sum(jnp.exp(values - peak[None, :]), axis=0), "src")
    return peak + jnp.log(total)


def on_device(src_embed, tgt_embed, qwen_embed, other_log, src_counts, tgt_counts):
    src_float = src_counts.astype(jnp.float32)
    tgt_float = tgt_counts.astype(jnp.float32)
    slab_sum = lax.psum(jnp.sum(src_float), "src")
    vocab_sum = lax.psum(jnp.sum(tgt_float), "tgt")
    src_log = jnp.log(src_float) - jnp.log(slab_sum)
    tgt_log = jnp.log(tgt_float) - jnp.log(vocab_sum)
    stored = logits_of(src_embed, tgt_embed)

    def current():
        return stored

    col_pot = jnp.zeros((tgt_embed.shape[0],), jnp.float32)
    row_pot = jnp.zeros((src_embed.shape[0],), jnp.float32)
    for sweep in range(ITERS):
        row_pot = src_log - row_lse(current() + col_pot[None, :])
        col_pot = tgt_log - jnp.logaddexp(col_lse(current() + row_pot[:, None]), other_log)
    shift = row_pot - src_log
    weights = jnp.exp(shift[:, None] + col_pot[None, :] + current()).astype(jnp.bfloat16)
    owned_rows = src_embed.shape[0] // lax.axis_size("tgt")
    partial_rows = jnp.dot(weights, qwen_embed, preferred_element_type=jnp.float32)
    summed = lax.psum(partial_rows, "tgt")
    return lax.dynamic_slice_in_dim(summed, lax.axis_index("tgt") * owned_rows, owned_rows, 0)


def solution(mesh):
    return jax.shard_map(
        on_device,
        mesh=mesh,
        in_specs=(P("src", None), P("tgt", None), P("tgt", None), P("tgt"), P("src"), P("tgt")),
        out_specs=P(("src", "tgt"), None),
        check_vma=False,
    )
```

profile of v0, /device:TPU:8, one launch (start us, length us, event | category | flops | bytes accessed | tf_op | source)
XLA Modules:
  0.0 646.8 jit_solution(11345955397474943461)
XLA Ops:
  6.5 0.0 copy-start
  6.5 0.0 all-reduce.3.cloned.1.call-start
  6.5 1.5 convert_reduce_fusion
  8.0 1.3 convert_reduce_fusion.1
  9.3 0.0 copy-done
  9.3 0.0 copy-start.3
  9.3 9.3 %fusion.4 = (f32[1024]{0:T(1024)S(1)}, f32[1024,4864]{1,0:T(8,128)}) fusion(bf16[1024,256]{1,0:T(8,128)(2,1)} %param.6, bf16[4864,256]{1,0:T(8,128)(2,1)S(1)} %copy-done), kind=kOutput, calls=%fused_computation.24 | convolution fusion | flops 2560097280 | bytes 22941696 | tf_op jit(solution)/shard_map/dot_general | solution.py:11
  18.7 77.7 %pmax.28 = f32[1024]{0:T(1024)S(1)} all-reduce(f32[1024]{0:T(1024)S(1)} %get-tuple-element.9), channel_id=1, replica_groups=mesh['src'=8,'tgt'=32] {'tgt'}, use_global_device_ids=true, to_apply=%region_5.0 | all-reduce | flops 1024 | bytes 8192 | tf_op jit(solution)/shard_map/pmax | solution.py:19
  96.3 10.6 %psum.49 = f32[]{:T(128)} all-reduce(f32[]{:T(128)} %convert_reduce_fusion.1), channel_id=1, replica_groups=mesh['src'=8,'tgt'=32] {'src'}, use_global_device_ids=true, to_apply=%region_1.0 | all-reduce | flops 1 | bytes 8 | tf_op jit(solution)/shard_map/psum | solution.py:34
  107.7 9.4 %exponential_reduce_fusion.3 = f32[1024]{0:T(1024)S(1)} fusion(f32[1024,4864]{1,0:T(8,128)} %get-tuple-element.10, f32[1024]{0:T(1024)S(1)} %pmax.28), kind=kLoop, calls=%fused_computation.4 | loop fusion | flops 9960448 | bytes 19931136 | tf_op jit(solution)/shard_map/reduce_sum | solution.py:20
  117.1 71.1 %all-reduce = (f32[1024]{0:T(1024)S(1)}, f32[]{:T(128)}) all-reduce(f32[1024]{0:T(1024)S(1)} %exponential_reduce_fusion.3, f32[]{:T(128)} %convert_reduce_fusion), channel_id=1, replica_groups=mesh['src'=8,'tgt'=32] {'tgt'}, use_global_device_ids=true, to_apply=%region_7.0 | all-reduce | flops 1025 | bytes 8200 | tf_op jit(solution)/shard_map/psum | solution.py:20
  188.2 0.0 copy-done.3
  188.2 0.0 copy-start.1
  188.2 0.0 copy-start.2
  188.2 8.3 %add_reduce_fusion.2 = f32[4864]{0:T(1024)S(1)} fusion(f32[1024,4864]{1,0:T(8,128)} %get-tuple-element.10, f32[1024]{0:T(1024)S(1)} %add_subtract_fusion.1), kind=kLoop, calls=%fused_computation.7 | loop fusion | flops 9956608 | bytes 19946496 | tf_op jit(solution)/shard_map/reduce_max | solution.py:25
  196.5 23.0 %pmax.29 = f32[4864]{0:T(1024)S(1)} all-reduce(f32[4864]{0:T(1024)S(1)} %add_reduce_fusion.2), channel_id=1, replica_groups=mesh['src'=8,'tgt'=32] {'src'}, use_global_device_ids=true, to_apply=%region_9.0 | all-reduce | flops 4864 | bytes 38912 | tf_op jit(solution)/shard_map/pmax | solution.py:26
  219.5 10.9 %exponential_reduce_fusion.2 = f32[4864]{0:T(1024)S(1)} fusion(f32[1024,4864]{1,0:T(8,128)} %get-tuple-element.10, f32[4864]{0:T(1024)S(1)} %pmax.29, f32[1024]{0:T(1024)S(1)} %add_subtract_fusion.1), kind=kLoop, calls=%fused_computation.3 | loop fusion | flops 14937344 | bytes 19965952 | tf_op jit(solution)/shard_map/reduce_sum | solution.py:27
  230.4 23.8 %psum.52 = f32[4864]{0:T(1024)S(1)} all-reduce(f32[4864]{0:T(1024)S(1)} %exponential_reduce_fusion.2), channel_id=1, replica_groups=mesh['src'=8,'tgt'=32] {'src'}, use_global_device_ids=true, to_apply=%region_11.0 | all-reduce | flops 4864 | bytes 38912 | tf_op jit(solution)/shard_map/psum | solution.py:27
  254.9 0.0 copy-done.1
  254.9 0.0 copy-done.2
  254.9 8.1 %add_reduce_fusion.1 = f32[1024]{0:T(1024)S(1)} fusion(f32[1024,4864]{1,0:T(8,128)} %get-tuple-element.10, f32[4864]{0:T(1024)S(1)} %select_subtract_fusion.1), kind=kLoop, calls=%fused_computation.6 | loop fusion | flops 9960448 | bytes 19946496 | tf_op jit(solution)/shard_map/reduce_max | solution.py:18
  263.0 71.6 %pmax.30 = f32[1024]{0:T(1024)S(1)} all-reduce(f32[1024]{0:T(1024)S(1)} %add_reduce_fusion.1), channel_id=1, replica_groups=mesh['src'=8,'tgt'=32] {'tgt'}, use_global_device_ids=true, to_apply=%region_13.0 | all-reduce | flops 1024 | bytes 8192 | tf_op jit(solution)/shard_map/pmax | solution.py:19
  334.6 10.0 %exponential_reduce_fusion.1 = f32[1024]{0:T(1024)S(1)} fusion(f32[1024,4864]{1,0:T(8,128)} %get-tuple-element.10, f32[1024]{0:T(1024)S(1)} %pmax.30, f32[4864]{0:T(1024)S(1)} %select_subtract_fusion.1), kind=kLoop, calls=%fused_computation.2 | loop fusion | flops 14941184 | bytes 19950592 | tf_op jit(solution)/shard_map/reduce_sum | solution.py:20
  344.7 69.6 %psum.53 = f32[1024]{0:T(1024)S(1)} all-reduce(f32[1024]{0:T(1024)S(1)} %exponential_reduce_fusion.1), channel_id=1, replica_groups=mesh['src'=8,'tgt'=32] {'tgt'}, use_global_device_ids=true, to_apply=%region_15.0 | all-reduce | flops 1024 | bytes 8192 | tf_op jit(solution)/shard_map/psum | solution.py:20
  414.3 8.3 %add_reduce_fusion = f32[4864]{0:T(1024)S(1)} fusion(f32[1024,4864]{1,0:T(8,128)} %get-tuple-element.10, f32[1024]{0:T(1024)S(1)} %get-tuple-element.8), kind=kLoop, calls=%fused_computation.5 | loop fusion | flops 9956608 | bytes 19946496 | tf_op jit(solution)/shard_map/reduce_max | solution.py:25
  422.6 23.6 %pmax.31 = f32[4864]{0:T(1024)S(1)} all-reduce(f32[4864]{0:T(1024)S(1)} %add_reduce_fusion), channel_id=1, replica_groups=mesh['src'=8,'tgt'=32] {'src'}, use_global_device_ids=true, to_apply=%region_17.0 | all-reduce | flops 4864 | bytes 38912 | tf_op jit(solution)/shard_map/pmax | solution.py:26
  446.2 10.9 %exponential_reduce_fusion = f32[4864]{0:T(1024)S(1)} fusion(f32[1024,4864]{1,0:T(8,128)} %get-tuple-element.10, f32[4864]{0:T(1024)S(1)} %pmax.31, f32[1024]{0:T(1024)S(1)} %get-tuple-element.8), kind=kLoop, calls=%fused_computation.1 | loop fusion | flops 14937344 | bytes 19965952 | tf_op jit(solution)/shard_map/reduce_sum | solution.py:27
  457.1 23.8 %psum.54 = f32[4864]{0:T(1024)S(1)} all-reduce(f32[4864]{0:T(1024)S(1)} %exponential_reduce_fusion), channel_id=1, replica_groups=mesh['src'=8,'tgt'=32] {'src'}, use_global_device_ids=true, to_apply=%region_19.0 | all-reduce | flops 4864 | bytes 38912 | tf_op jit(solution)/shard_map/psum | solution.py:27
  480.9 11.5 %fusion = f32[1024,256]{1,0:T(8,128)} fusion(bf16[4864,256]{1,0:T(8,128)(2,1)} %param.8, f32[1024,4864]{1,0:T(8,128)} %get-tuple-element.10, f32[4864]{0:T(1024)S(1)} %select_subtract_fusion, f32[1024]{0:T(1024)S(1)} %get-tuple-element.7), kind=kOutput, calls=%fused_computation.9 | convolution fusion | flops 2565079040 | bytes 23485440 | tf_op jit(solution)/shard_map/dot_general | solution.py:51
  492.4 0.0 all-reduce.3.cloned.1.call-update
  492.5 146.1 %all-reduce.3.cloned.1.call-done = f32[1024,256]{1,0:T(8,128)} async-done(((f32[1024,256]{1,0:T(8,128)}), f32[1024,256]{1,0:T(8,128)}) %all-reduce.3.cloned.1.call-update) | async-done | bytes 1048592 | tf_op jit(solution)/shard_map/psum | solution.py:52
  638.6 1.4 constant_dynamic-slice_fusion
  (4 shorter events, 0.1 us)
Async XLA Ops:
  6.5 2.8 copy-start
  6.5 632.0 %all-reduce.3.cloned.1.call-start = ((), (), s32[]{:S(2)}) async-start(), calls=%async_computation | async-start | bytes 2097152 | tf_op jit(solution)/shard_map/psum | solution.py:52
  9.3 178.9 %copy-start.3 = (s32[1024]{0:T(1024)S(1)}, s32[1024]{0:T(1024)}, u32[]{:S(2)}) copy-start(s32[1024]{0:T(1024)} %param.10) | copy-start | bytes 12292
  188.2 66.7 %copy-start.1 = (s32[4864]{0:T(1024)S(1)}, s32[4864]{0:T(1024)}, u32[]{:S(2)}) copy-start(s32[4864]{0:T(1024)} %param.11) | copy-start | bytes 58372
  188.2 66.7 %copy-start.2 = (f32[4864]{0:T(1024)S(1)}, f32[4864]{0:T(1024)}, u32[]{:S(2)}) copy-start(f32[4864]{0:T(1024)} %param.9) | copy-start | bytes 58372
Sparse Core Ops, SparseCore 0:
  492.6 145.9 all-reduce.2
where the time goes:
time: 647 us
  blocking collectives  395 us (61%)
  waiting for transfers between devices  146 us (23%)
  other arithmetic  68.7 us (11%)
  matrix products  20.8 us (3%)
  between operations  14.8 us (2%)
    pmax x2, blocking collectives, row_lse(): peak = lax.pmax(local_peak, 'tgt')  149 us
    psum x1, waiting for transfers between devices, on_device(): summed = lax.psum(partial_rows, 'tgt')  146 us
    psum x2, blocking collectives, row_lse(): total = lax.psum(jnp.sum(jnp.exp(values - peak[:, None]), axis=1), 'tgt')  141 us
    psum x2, blocking collectives, col_lse(): total = lax.psum(jnp.sum(jnp.exp(values - peak[None, :]), axis=0), 'src')  47.6 us
    pmax x2, blocking collectives, col_lse(): peak = lax.pmax(local_peak, 'src')  46.6 us
    reduce_sum x2, other arithmetic, col_lse(): total = lax.psum(jnp.sum(jnp.exp(values - peak[None, :]), axis=0), 'src')  21.7 us
    reduce_sum x2, other arithmetic, row_lse(): total = lax.psum(jnp.sum(jnp.exp(values - peak[:, None]), axis=1), 'tgt')  19.4 us
    reduce_max x2, other arithmetic, col_lse(): local_peak = jnp.max(values, axis=0)  16.6 us
  transfers between devices with their start and end apart: 1, of which 1 were waited for; matrix products, arithmetic and copies ran while one was open for 0% of the time, Pallas kernels for 0%

commit v1 on v0

--- a/solution.py
+++ b/solution.py
@@ -24,7 +24,7 @@
 def col_lse(values):
     local_peak = jnp.max(values, axis=0)
     peak = lax.pmax(local_peak, "src")
-    total = lax.psum(jnp.sum(jnp.exp(values - peak[None, :]), axis=0), "src")
+    total = jnp.sum(lax.all_gather(jnp.sum(jnp.exp(values - peak[None, :]), axis=0), "src"), axis=0)
     return peak + jnp.log(total)
 
 

time: 647 us -> 627 us (0.969)
  blocking collectives: 395 us -> 374 us
    psum x2 -> x0, blocking collectives: 47.6 us -> none  [col_lse(): total = lax.psum(jnp.sum(jnp.exp(values - peak[None, :]), axis=0), 'src')]
    all_gather x0 -> x2, blocking collectives: none -> 26.3 us  [col_lse(): lax.all_gather(jnp.sum(jnp.exp(values - peak[None, :]), axis=0), 'src')]
    reduce_sum x2 -> x4, other arithmetic: 21.7 us -> 22 us  [the longest x2 21.7 us: col_lse(): jnp.sum(jnp.exp(values - peak[None, :]), axis=0)]
where the time goes in v1:
time: 627 us; the launch traced here: 626 us
  blocking collectives  374 us (60%)
  waiting for transfers between devices  147 us (23%)
  other arithmetic  68.9 us (11%)
  matrix products  20.8 us (3%)
  between operations  14.9 us (2%)
    pmax x2, blocking collectives, row_lse(): peak = lax.pmax(local_peak, 'tgt')  149 us
    psum x1, waiting for transfers between devices, on_device(): summed = lax.psum(partial_rows, 'tgt')  147 us
    psum x2, blocking collectives, row_lse(): total = lax.psum(jnp.sum(jnp.exp(values - peak[:, None]), axis=1), 'tgt')  141 us
    pmax x2, blocking collectives, col_lse(): peak = lax.pmax(local_peak, 'src')  46.5 us
    all_gather x2, blocking collectives, col_lse(): lax.all_gather(jnp.sum(jnp.exp(values - peak[None, :]), axis=0), 'src')  26.3 us
    reduce_sum x2, other arithmetic, col_lse(): jnp.sum(jnp.exp(values - peak[None, :]), axis=0)  21.7 us
    reduce_sum x2, other arithmetic, row_lse(): total = lax.psum(jnp.sum(jnp.exp(values - peak[:, None]), axis=1), 'tgt')  19.4 us
    reduce_max x2, other arithmetic, col_lse(): local_peak = jnp.max(values, axis=0)  16.6 us
  transfers between devices with their start and end apart: 1, of which 1 were waited for; matrix products, arithmetic and copies ran while one was open for 0% of the time, Pallas kernels for 0%

profile of v1, /device:TPU:8, one launch (start us, length us, event | category | flops | bytes accessed | tf_op | source)
XLA Modules:
  0.0 626.4 jit_solution(881737695912126949)
XLA Ops:
  6.5 0.0 copy-start
  6.5 0.0 all-reduce.3.cloned.1.call-start
  6.5 1.5 convert_reduce_fusion
  8.0 1.3 convert_reduce_fusion.1
  9.3 0.0 copy-done
  9.3 9.3 %fusion.4 = (f32[1024]{0:T(1024)S(1)}, f32[1024,4864]{1,0:T(8,128)}) fusion(bf16[1024,256]{1,0:T(8,128)(2,1)} %param.6, bf16[4864,256]{1,0:T(8,128)(2,1)S(1)} %copy-done), kind=kOutput, calls=%fused_computation.24 | convolution fusion | flops 2560097280 | bytes 22941696 | tf_op jit(solution)/shard_map/dot_general | solution.py:11
  18.7 77.7 %pmax.28 = f32[1024]{0:T(1024)S(1)} all-reduce(f32[1024]{0:T(1024)S(1)} %get-tuple-element.9), channel_id=1, replica_groups=mesh['src'=8,'tgt'=32] {'tgt'}, use_global_device_ids=true, to_apply=%region_5.0 | all-reduce | flops 1024 | bytes 8192 | tf_op jit(solution)/shard_map/pmax | solution.py:19
  96.3 10.6 %psum.35 = f32[]{:T(128)} all-reduce(f32[]{:T(128)} %convert_reduce_fusion.1), channel_id=1, replica_groups=mesh['src'=8,'tgt'=32] {'src'}, use_global_device_ids=true, to_apply=%region_1.0 | all-reduce | flops 1 | bytes 8 | tf_op jit(solution)/shard_map/psum | solution.py:34
  107.7 9.4 %exponential_reduce_fusion.3 = f32[1024]{0:T(1024)S(1)} fusion(f32[1024,4864]{1,0:T(8,128)} %get-tuple-element.10, f32[1024]{0:T(1024)S(1)} %pmax.28), kind=kLoop, calls=%fused_computation.4 | loop fusion | flops 9960448 | bytes 19931136 | tf_op jit(solution)/shard_map/reduce_sum | solution.py:20
  117.1 71.1 %all-reduce = (f32[1024]{0:T(1024)S(1)}, f32[]{:T(128)}) all-reduce(f32[1024]{0:T(1024)S(1)} %exponential_reduce_fusion.3, f32[]{:T(128)} %convert_reduce_fusion), channel_id=1, replica_groups=mesh['src'=8,'tgt'=32] {'tgt'}, use_global_device_ids=true, to_apply=%region_7.0 | all-reduce | flops 1025 | bytes 8200 | tf_op jit(solution)/shard_map/psum | solution.py:20
  188.2 0.0 copy-start.1
  188.2 0.0 copy-start.2
  188.2 8.3 %add_reduce_fusion.2 = f32[4864]{0:T(1024)S(1)} fusion(f32[1024,4864]{1,0:T(8,128)} %get-tuple-element.10, f32[1024]{0:T(1024)S(1)} %add_subtract_fusion.1), kind=kLoop, calls=%fused_computation.7 | loop fusion | flops 9956608 | bytes 19946496 | tf_op jit(solution)/shard_map/reduce_max | solution.py:25
  196.5 23.0 %pmax.29 = f32[4864]{0:T(1024)S(1)} all-reduce(f32[4864]{0:T(1024)S(1)} %add_reduce_fusion.2), channel_id=1, replica_groups=mesh['src'=8,'tgt'=32] {'src'}, use_global_device_ids=true, to_apply=%region_9.0 | all-reduce | flops 4864 | bytes 38912 | tf_op jit(solution)/shard_map/pmax | solution.py:26
  219.5 10.9 %exponential_reduce_fusion.2 = f32[4864]{0:T(1024)S(1)} fusion(f32[1024,4864]{1,0:T(8,128)} %get-tuple-element.10, f32[4864]{0:T(1024)S(1)} %pmax.29, f32[1024]{0:T(1024)S(1)} %add_subtract_fusion.1), kind=kLoop, calls=%fused_computation.3 | loop fusion | flops 14937344 | bytes 19965952 | tf_op jit(solution)/shard_map/reduce_sum | solution.py:27
  230.4 13.2 %all-gather.2 = f32[8,1,4864]{2,1,0:T(1,128)S(1)} all-gather(f32[1,1,4864]{2,1,0:T(1,128)S(1)} %reshape.11), channel_id=2, replica_groups=mesh['src'=8,'tgt'=32] {'src'}, dimensions={0}, use_global_device_ids=true | all-gather | bytes 175104 | tf_op jit(solution)/shard_map/all_gather | solution.py:27
  244.4 0.1 reduce_sum.76
  244.5 0.0 copy-done.1
  244.5 0.0 copy-done.2
  244.6 8.1 %add_reduce_fusion.1 = f32[1024]{0:T(1024)S(1)} fusion(f32[1024,4864]{1,0:T(8,128)} %get-tuple-element.10, f32[4864]{0:T(1024)S(1)} %select_subtract_fusion.1), kind=kLoop, calls=%fused_computation.6 | loop fusion | flops 9960448 | bytes 19946496 | tf_op jit(solution)/shard_map/reduce_max | solution.py:18
  252.6 71.6 %pmax.30 = f32[1024]{0:T(1024)S(1)} all-reduce(f32[1024]{0:T(1024)S(1)} %add_reduce_fusion.1), channel_id=1, replica_groups=mesh['src'=8,'tgt'=32] {'tgt'}, use_global_device_ids=true, to_apply=%region_13.0 | all-reduce | flops 1024 | bytes 8192 | tf_op jit(solution)/shard_map/pmax | solution.py:19
  324.2 10.0 %exponential_reduce_fusion.1 = f32[1024]{0:T(1024)S(1)} fusion(f32[1024,4864]{1,0:T(8,128)} %get-tuple-element.10, f32[1024]{0:T(1024)S(1)} %pmax.30, f32[4864]{0:T(1024)S(1)} %select_subtract_fusion.1), kind=kLoop, calls=%fused_computation.2 | loop fusion | flops 14941184 | bytes 19950592 | tf_op jit(solution)/shard_map/reduce_sum | solution.py:20
  334.3 69.7 %psum.38 = f32[1024]{0:T(1024)S(1)} all-reduce(f32[1024]{0:T(1024)S(1)} %exponential_reduce_fusion.1), channel_id=1, replica_groups=mesh['src'=8,'tgt'=32] {'tgt'}, use_global_device_ids=true, to_apply=%region_15.0 | all-reduce | flops 1024 | bytes 8192 | tf_op jit(solution)/shard_map/psum | solution.py:20
  403.9 8.3 %add_reduce_fusion = f32[4864]{0:T(1024)S(1)} fusion(f32[1024,4864]{1,0:T(8,128)} %get-tuple-element.10, f32[1024]{0:T(1024)S(1)} %get-tuple-element.8), kind=kLoop, calls=%fused_computation.5 | loop fusion | flops 9956608 | bytes 19946496 | tf_op jit(solution)/shard_map/reduce_max | solution.py:25
  412.2 23.5 %pmax.31 = f32[4864]{0:T(1024)S(1)} all-reduce(f32[4864]{0:T(1024)S(1)} %add_reduce_fusion), channel_id=1, replica_groups=mesh['src'=8,'tgt'=32] {'src'}, use_global_device_ids=true, to_apply=%region_17.0 | all-reduce | flops 4864 | bytes 38912 | tf_op jit(solution)/shard_map/pmax | solution.py:26
  435.7 10.9 %exponential_reduce_fusion = f32[4864]{0:T(1024)S(1)} fusion(f32[1024,4864]{1,0:T(8,128)} %get-tuple-element.10, f32[4864]{0:T(1024)S(1)} %pmax.31, f32[1024]{0:T(1024)S(1)} %get-tuple-element.8), kind=kLoop, calls=%fused_computation.1 | loop fusion | flops 14937344 | bytes 19965952 | tf_op jit(solution)/shard_map/reduce_sum | solution.py:27
  446.6 13.1 %all-gather.3 = f32[8,1,4864]{2,1,0:T(1,128)S(1)} all-gather(f32[1,1,4864]{2,1,0:T(1,128)S(1)} %reshape.13), channel_id=3, replica_groups=mesh['src'=8,'tgt'=32] {'src'}, dimensions={0}, use_global_device_ids=true | all-gather | bytes 175104 | tf_op jit(solution)/shard_map/all_gather | solution.py:27
  459.7 0.1 reduce_sum.79
  459.9 11.5 %fusion = f32[1024,256]{1,0:T(8,128)} fusion(bf16[4864,256]{1,0:T(8,128)(2,1)} %param.8, f32[1024,4864]{1,0:T(8,128)} %get-tuple-element.10, f32[4864]{0:T(1024)S(1)} %select_subtract_fusion, f32[1024]{0:T(1024)S(1)} %get-tuple-element.7), kind=kOutput, calls=%fused_computation.9 | convolution fusion | flops 2565079040 | bytes 23485440 | tf_op jit(solution)/shard_map/dot_general | solution.py:51
  471.4 0.0 all-reduce.3.cloned.1.call-update
  471.4 146.8 %all-reduce.3.cloned.1.call-done = f32[1024,256]{1,0:T(8,128)} async-done(((f32[1024,256]{1,0:T(8,128)}), f32[1024,256]{1,0:T(8,128)}) %all-reduce.3.cloned.1.call-update) | async-done | bytes 1048592 | tf_op jit(solution)/shard_map/psum | solution.py:52
  618.2 1.4 constant_dynamic-slice_fusion
  (8 shorter events, 0.1 us)
Async XLA Ops:
  6.5 2.8 copy-start
  6.5 611.7 %all-reduce.3.cloned.1.call-start = ((), (), s32[]{:S(2)}) async-start(), calls=%async_computation | async-start | bytes 2097152 | tf_op jit(solution)/shard_map/psum | solution.py:52
  9.3 178.9 %copy-start.3 = (s32[1024]{0:T(1024)S(1)}, s32[1024]{0:T(1024)}, u32[]{:S(2)}) copy-start(s32[1024]{0:T(1024)} %param.10) | copy-start | bytes 12292
  188.2 56.3 %copy-start.1 = (s32[4864]{0:T(1024)S(1)}, s32[4864]{0:T(1024)}, u32[]{:S(2)}) copy-start(s32[4864]{0:T(1024)} %param.11) | copy-start | bytes 58372
  188.2 56.3 %copy-start.2 = (f32[4864]{0:T(1024)S(1)}, f32[4864]{0:T(1024)}, u32[]{:S(2)}) copy-start(f32[4864]{0:T(1024)} %param.9) | copy-start | bytes 58372
Sparse Core Ops, SparseCore 0:
  471.5 146.6 all-reduce.2
